TPU v7x, 32 devices: a whole 2x2x4 slice. The times are simulated.
32 devices in a mesh: dp: 16 (over z, y, core), mp: 2 (over x).
Axes of the slice: x: 2, y: 2, z: 4, core: 2. Of those that a mesh axis runs over, the one named last changes fastest.
Arguments:
- features: bfloat16 [2048, 4608], P('dp'), may hold values from -6 to 6
- proj_in: bfloat16 [4608, 2560], P('dp', 'mp'), may hold values from -0.09375 to 0.09375
- proj_out: bfloat16 [2560, 2560], P('mp'), may hold values from -0.125 to 0.125
- expert_gate: bfloat16 [64, 2560, 1536], P('dp', None, 'mp'), may hold values from -0.125 to 0.125
- expert_up: bfloat16 [64, 2560, 1536], P('dp', None, 'mp'), may hold values from -0.125 to 0.125
- expert_down: bfloat16 [64, 1536, 2560], P('dp', 'mp'), may hold values from -0.15625 to 0.15625
- routes: int32 [2048, 6], P('dp'), may hold values from 0 to 63, all different within a row; in each aligned block of 128 rows (0 to 127, 128 to 255, ...) at most 15 rows name the same one
- gate_weights: float32 [2048, 6], P('dp'), may hold values from 0.1 to 0.6
- cotangent: bfloat16 [2048, 2560], P('dp'), may hold values from -0.09375 to 0.09375
- first_in: float32 [4608, 2560], P('dp', 'mp'), may hold values from -2 to 2
- second_in: float32 [4608, 2560], P('dp', 'mp'), may hold values from 0.02 to 1
- first_out: float32 [2560, 2560], P('mp', 'dp'), may hold values from -2 to 2
- second_out: float32 [2560, 2560], P('mp', 'dp'), may hold values from 0.02 to 1
Outputs:
- moe_out: bfloat16 [2048, 2560], P('dp')
- new_proj_in: bfloat16 [4608, 2560], P('dp', 'mp')
- new_proj_out: bfloat16 [2560, 2560], P('mp', 'dp')
- new_first_in: float32 [4608, 2560], P('dp', 'mp')
- new_second_in: float32 [4608, 2560], P('dp', 'mp')
- new_first_out: float32 [2560, 2560], P('mp', 'dp')
- new_second_out: float32 [2560, 2560], P('mp', 'dp')
Inputs may be any that keep to these rules, and one draw needn't show every extreme that they name: `routes`: each row names 6 different experts. Within the rows of one device (aligned blocks of 128 rows) no expert is named more than 15 times, and in every draw some expert is named exactly 15 times in some block.
All inputs are finite; a program needn't handle non-finite values.
Results may differ from a plain program's by a relative error of at most 0.01.
Values may be sent and summed in bfloat16 or wider, within the bound.
A program may use at most 192 MiB of HBM per device.

v0:
```python
import jax
import jax.numpy as jnp
from jax import lax
from jax.sharding import PartitionSpec as P

EXPERTS = 64
TOP = 6
CAP = 15


BETA_ONE = 0.9
BETA_TWO = 0.999
EPSILON = 1e-08
LEARN_RATE = 0.001
WEIGHT_DECAY = 0.1
FIRST_FIX = 1.0 - 0.9**50 * 0.9**50
SECOND_FIX = 1.0 - 0.999**50 * 0.999**50


def gelu_parts(preact):

    def smooth(values):
        return jax.nn.gelu(values, approximate=True)

    result, pullback = jax.vjp(smooth, preact)
    return (result, pullback(jnp.ones_like(preact))[0])


def slot_table(chosen_block):
    chosen = chosen_block.reshape(-1)
    onehot = (chosen[:, None] == jnp.arange(EXPERTS, dtype=jnp.int32)[None, :]).astype(jnp.int32)
    earlier = jnp.cumsum(onehot, axis=0) - onehot
    return (chosen, jnp.sum(earlier * onehot, axis=1))


def adamw_update(weight, gradient, first, second):
    first_new = BETA_ONE * first + (1.0 - BETA_ONE) * gradient
    second_new = BETA_TWO * second + (1.0 - BETA_TWO) * gradient * gradient
    update = first_new / FIRST_FIX / (jnp.sqrt(second_new / SECOND_FIX) + EPSILON)
    current = weight.astype(jnp.float32)
    return (
        (current - LEARN_RATE * (update + WEIGHT_DECAY * current)).astype(jnp.bfloat16),
        first_new,
        second_new,
    )


def expert_pass(inputs, grads_in, w_gate, w_up, w_down):
    gate_projection = jnp.einsum("erd,edf->erf", inputs, w_gate, preferred_element_type=jnp.float32)
    up_projection = jnp.einsum("erd,edf->erf", inputs, w_up, preferred_element_type=jnp.float32)
    sigmoid_gate = jax.nn.sigmoid(gate_projection)
    silu_gate = gate_projection * sigmoid_gate
    inner_activation = (silu_gate * up_projection).astype(jnp.bfloat16)
    out_part = jnp.einsum(
        "erf,efd->erd", inner_activation, w_down, preferred_element_type=jnp.float32
    ).astype(jnp.bfloat16)
    down_weight_gradient = jnp.einsum(
        "erd,efd->erf", grads_in, w_down, preferred_element_type=jnp.float32
    )
    gate_weight_gradient = (
        down_weight_gradient
        * up_projection
        * sigmoid_gate
        * (1.0 + gate_projection * (1.0 - sigmoid_gate))
    ).astype(jnp.bfloat16)
    up_weight_gradient = (down_weight_gradient * silu_gate).astype(jnp.bfloat16)
    input_part = (
        jnp.einsum("erf,edf->erd", gate_weight_gradient, w_gate, preferred_element_type=jnp.float32)
        + jnp.einsum("erf,edf->erd", up_weight_gradient, w_up, preferred_element_type=jnp.float32)
    ).astype(jnp.bfloat16)
    return (out_part, input_part)


def slot_sources(position, flat_weights, total_slots):
    pair_count = position.shape[0]
    owner = (
        jnp.zeros((total_slots,), jnp.int32)
        .at[position]
        .set(jnp.arange(pair_count, dtype=jnp.int32) + 1)
    )
    live = owner > 0
    pair_id = jnp.maximum(owner - 1, 0)
    source_row = pair_id // TOP
    slot_weight = jnp.where(live, flat_weights[pair_id], 0.0)
    return (live, source_row, slot_weight)


def fill_inputs(rows, live, source_row):
    return jnp.where(live[:, None], rows[source_row], jnp.zeros((), rows.dtype))


def fill_grads(grads, slot_weight, source_row):
    return (slot_weight[:, None] * grads[source_row].astype(jnp.float32)).astype(jnp.bfloat16)


def collect_rows(buffer, pair_slots, pair_weights):
    flat = buffer.reshape(-1, buffer.shape[-1])
    total = jnp.zeros((pair_slots.shape[0], flat.shape[1]), jnp.float32)
    for choice_index in range(TOP):
        picked = flat[pair_slots[:, choice_index]].astype(jnp.float32)
        if pair_weights is None:
            total = total + picked
        else:
            total = total + pair_weights[:, choice_index : choice_index + 1] * picked
    return total


def embed_columns(columns, column_start, model_width):
    canvas = jnp.zeros((columns.shape[0], model_width), jnp.float32)
    return lax.dynamic_update_slice_in_dim(canvas, columns.astype(jnp.float32), column_start, 1)


def local(
    features,
    proj_in,
    proj_out,
    expert_gate,
    expert_up,
    expert_down,
    routes,
    gate_weights,
    cotangent,
    first_in,
    second_in,
    first_out,
    second_out,
):
    row_count = features.shape[0]
    model_width = cotangent.shape[1]
    data_parts = lax.axis_size("dp")
    model_parts = lax.axis_size("mp")
    data_place = lax.axis_index("dp")
    model_place = lax.axis_index("mp")
    column_width = model_width // model_parts
    column_start = model_place * column_width
    own_experts = expert_gate.shape[0]
    total_slots = own_experts * data_parts * CAP
    expert_rows = data_parts * CAP
    preact = jnp.dot(
        features,
        lax.all_gather(proj_in, "dp", axis=0, tiled=True),
        preferred_element_type=jnp.float32,
    )
    activated, gelu_slope = gelu_parts(preact)
    hidden = activated.astype(jnp.bfloat16)
    partial_value = jnp.dot(hidden, proj_out, preferred_element_type=jnp.float32)
    chosen, slot_index = slot_table(routes)
    position = chosen * CAP + slot_index
    pair_slots = position.reshape(row_count, TOP)
    live, source_row, slot_weight = slot_sources(position, gate_weights.reshape(-1), total_slots)
    cotangent_cols = lax.dynamic_slice_in_dim(cotangent, column_start, column_width, 1)
    mapped_cols = lax.psum_scatter(partial_value, "mp", scatter_dimension=1, tiled=True).astype(
        jnp.bfloat16
    )
    send_rows = fill_inputs(mapped_cols, live, source_row)
    send_grads = fill_grads(cotangent_cols, slot_weight, source_row)
    send_shape = (data_parts, own_experts, CAP, column_width)
    narrow_rows, narrow_grads = (
        lax.all_to_all(
            send_rows.reshape(send_shape), "dp", split_axis=0, concat_axis=2, tiled=True
        ),
        lax.all_to_all(
            send_grads.reshape(send_shape), "dp", split_axis=0, concat_axis=2, tiled=True
        ),
    )
    recv_rows, recv_grads = (
        lax.all_gather(narrow_rows, "mp", axis=3, tiled=True),
        lax.all_gather(narrow_grads, "mp", axis=3, tiled=True),
    )
    out_part, input_part = expert_pass(
        recv_rows.reshape(own_experts, expert_rows, model_width),
        recv_grads.reshape(own_experts, expert_rows, model_width),
        expert_gate,
        expert_up,
        expert_down,
    )
    back_shape = (1, own_experts, expert_rows, model_width)
    back_out, back_in = (
        lax.all_to_all(out_part.reshape(back_shape), "dp", split_axis=2, concat_axis=0, tiled=True),
        lax.all_to_all(
            input_part.reshape(back_shape), "dp", split_axis=2, concat_axis=0, tiled=True
        ),
    )
    out_terms = collect_rows(back_out, pair_slots, gate_weights) + embed_columns(
        mapped_cols, column_start, model_width
    )
    grad_terms_sum = collect_rows(back_in, pair_slots, None) + embed_columns(
        cotangent_cols, column_start, model_width
    )
    total_out, total_in = lax.psum((out_terms, grad_terms_sum), "mp")
    moe_out = total_out.astype(jnp.bfloat16)
    grad_mapped = total_in.astype(jnp.bfloat16)
    grad_hidden = lax.dot_general(
        grad_mapped, proj_out, (((1,), (1,)), ((), ())), preferred_element_type=jnp.float32
    )
    grad_pre = (grad_hidden * gelu_slope).astype(jnp.bfloat16)
    vis_part = features.shape[1] // data_parts
    width_part = model_width // data_parts
    share_rows = vis_part + width_part
    feature_blocks = features.reshape(row_count, data_parts, vis_part)
    mapped_blocks = grad_mapped.reshape(row_count, data_parts, width_part)
    term_in = jnp.einsum(
        "tnv,th->nvh", feature_blocks, grad_pre, preferred_element_type=jnp.float32
    )
    term_out = jnp.einsum("tnd,th->ndh", mapped_blocks, hidden, preferred_element_type=jnp.float32)
    shares = lax.psum_scatter(
        jnp.concatenate([term_in, term_out], axis=1)
        .reshape(share_rows * lax.axis_size("dp"), hidden.shape[1])
        .astype(jnp.bfloat16),
        "dp",
        scatter_dimension=0,
        tiled=True,
    ).astype(jnp.float32)
    grad_in = shares[:vis_part]
    grad_out = shares[vis_part:].T
    own_out = lax.dynamic_slice_in_dim(proj_out, data_place * width_part, width_part, 1)
    new_in, first_in_new, second_in_new = adamw_update(proj_in, grad_in, first_in, second_in)
    new_out, first_out_new, second_out_new = adamw_update(own_out, grad_out, first_out, second_out)
    return (moe_out, new_in, new_out, first_in_new, second_in_new, first_out_new, second_out_new)


def solution(mesh):
    return jax.shard_map(
        local,
        mesh=mesh,
        in_specs=(
            P("dp", None),
            P("dp", "mp"),
            P("mp", None),
            P("dp", None, "mp"),
            P("dp", None, "mp"),
            P("dp", "mp", None),
            P("dp", None),
            P("dp", None),
            P("dp", None),
            P("dp", "mp"),
            P("dp", "mp"),
            P("mp", "dp"),
            P("mp", "dp"),
        ),
        out_specs=(
            P("dp", None),
            P("dp", "mp"),
            P("mp", "dp"),
            P("dp", "mp"),
            P("dp", "mp"),
            P("mp", "dp"),
            P("mp", "dp"),
        ),
        check_vma=False,
    )
```

profile of v0, /device:TPU:0, one launch (start us, length us, event | category | flops | bytes accessed | tf_op | source)
XLA Modules:
  0.0 937.0 jit_solution(17657232542428289778)
XLA Ops:
  7.9 100.7 %all-gather.4.cloned.1.call-done = bf16[4608,1280]{1,0:T(8,128)(2,1)} async-done(((bf16[288,1280]{1,0:T(8,128)(2,1)}), bf16[4608,1280]{1,0:T(8,128)(2,1)}) %all-gather.4.cloned.1.call-update) | async-done | bytes 11796496 | tf_op jit(solution)/shard_map/all_gather | solution.py:141
  108.6 6.4 fusion.52
  131.4 10.4 %reduce-scatter.3.cloned.1.call-done = f32[128,1280]{1,0:T(8,128)} async-done(((f32[128,2560]{1,0:T(8,128)}), f32[128,1280]{1,0:T(8,128)}) %reduce-scatter.3.cloned.1.call-update) | async-done | bytes 655376 | tf_op jit(solution)/shard_map/reduce_scatter | solution.py:152
  152.8 61.0 %all_to_all.66 = bf16[16,4,15,1280]{3,1,2,0:T(4,128)(2,1)S(1)} all-to-all(bf16[16,4,15,1280]{3,1,2,0:T(4,128)(2,1)S(1)} %copy.63), channel_id=1, replica_groups=mesh['dp'=16,'mp'=2] {'dp'}, dimensions={0} | all-to-all | bytes 4915200 | tf_op jit(solution)/shard_map/all_to_all | solution.py:159
  234.2 45.3 %all-gather.6.cloned.1.call-done = bf16[1,4,240,2560]{3,2,1,0:T(8,128)(2,1)} async-done(((bf16[1,4,240,1280]{3,2,1,0:T(8,128)(2,1)}), bf16[1,4,240,2560]{3,2,1,0:T(8,128)(2,1)}) %all-gather.6.cloned.1.call-update) | async-done | bytes 4915216 | tf_op jit(solution)/shard_map/all_gather | solution.py:167
  279.5 12.7 %fusion.3 = f32[4,240,768]{2,1,0:T(8,128)} fusion(bf16[4,2560,768]{2,1,0:T(8,128)(2,1)} %param.17, bf16[1,4,240,2560]{3,2,1,0:T(8,128)(2,1)} %all-gather.6.cloned.1.call-done), kind=kOutput, calls=%fused_computation.25 | convolution fusion | flops 3774873600 | bytes 23592960 | tf_op jit(solution)/shard_map/erd,edf->erf/dot_general | solution.py:50
  292.3 7.6 fusion.5
  299.8 13.6 %fusion.7 = bf16[1,4,240,2560]{3,2,1,0:T(8,128)(2,1)} fusion(bf16[4,768,2560]{2,1,0:T(8,128)(2,1)} %param.18, f32[4,240,768]{2,1,0:T(8,128)} %fusion.3, f32[4,240,768]{2,1,0:T(8,128)S(1)} %fusion.5), kind=kOutput, calls=%fused_computation.29 | convolution fusion | flops 3781754880 | bytes 26542080 | tf_op jit(solution)/shard_map/erf,efd->erd/dot_general | solution.py:54
  313.5 8.4 copy.65
  327.6 12.8 %all-gather.8.cloned.1.call-start = ((), (), s32[]{:S(2)}) async-start(), calls=%async_computation.9 | async-start | bytes 7372800 | tf_op jit(solution)/shard_map/all_gather | solution.py:168
  342.2 65.3 %all-gather.8.cloned.1.call-done = bf16[1,4,240,2560]{3,2,1,0:T(8,128)(2,1)} async-done(((bf16[1,4,240,1280]{3,2,1,0:T(8,128)(2,1)}), bf16[1,4,240,2560]{3,2,1,0:T(8,128)(2,1)}) %all-gather.8.cloned.1.call-update) | async-done | bytes 4915216 | tf_op jit(solution)/shard_map/all_gather | solution.py:168
  407.5 12.8 %fusion.1 = f32[4,240,768]{2,1,0:T(8,128)} fusion(bf16[4,768,2560]{2,1,0:T(8,128)(2,1)} %param.18, bf16[1,4,240,2560]{3,2,1,0:T(8,128)(2,1)} %all-gather.8.cloned.1.call-done), kind=kOutput, calls=%fused_computation.23 | convolution fusion | flops 3774873600 | bytes 23592960 | tf_op jit(solution)/shard_map/erd,efd->erf/dot_general | solution.py:57
  420.3 13.0 %fusion.16 = f32[4,240,2560]{2,1,0:T(8,128)} fusion(bf16[4,2560,768]{2,1,0:T(8,128)(2,1)} %param.16, f32[4,240,768]{2,1,0:T(8,128)} %copy-done.2, f32[4,240,768]{2,1,0:T(8,128)} %fusion.1, f32[4,240,768]{2,1,0:T(8,128)} %fusion.3), kind=kOutput, calls=%fused_computation.47 | convolution fusion | flops 3782246400 | bytes 34406400 | tf_op jit(solution)/shard_map/erf,edf->erd/dot_general | solution.py:68
  433.3 14.6 %fusion.8 = bf16[1,4,240,2560]{3,2,1,0:T(8,128)(2,1)} fusion(f32[4,240,2560]{2,1,0:T(8,128)} %fusion.16, bf16[4,2560,768]{2,1,0:T(8,128)(2,1)} %param.17, f32[4,240,768]{2,1,0:T(8,128)} %fusion.1, f32[4,240,768]{2,1,0:T(8,128)} %copy-done.2), kind=kOutput, calls=%fused_computation.30 | convolution fusion | flops 3784212480 | bytes 36372480 | tf_op jit(solution)/shard_map/erf,edf->erd/dot_general | solution.py:69
  447.9 8.5 copy.70
  456.4 5.8 all-to-all-start.3
  464.0 5.9 copy.66
  469.9 7.6 reshape.114
  486.8 65.5 %all-to-all-done.3 = bf16[1,4,240,2560]{3,1,0,2:T(4,128)(2,1)} async-done(((bf16[1,4,240,2560]{3,1,0,2:T(4,128)(2,1)}), bf16[1,4,240,2560]{3,1,0,2:T(4,128)(2,1)}, u32[]{:S(2)}, u32[]{:S(2)}) %all-to-all-start.3) | async-done | bytes 4915232 | tf_op jit(solution)/shard_map/all_to_all | solution.py:180
  552.3 6.0 copy.71
  558.3 8.0 reshape.118
  625.6 66.1 %all-reduce.2 = (bf16[128,2560]{1,0:T(8,128)(2,1)}, bf16[128,2560]{1,0:T(8,128)(2,1)}) all-reduce(f32[128,2560]{1,0:T(8,128)S(1)} %add_dynamic-update-slice_fusion.1, f32[128,2560]{1,0:T(8,128)S(1)} %add_dynamic-update-slice_fusion), channel_id=1, replica_groups=mesh['dp'=16,'mp'=2] {'mp'}, use_global_device_ids=true, to_apply=%region_5.6 | all-reduce | flops 655360 | bytes 3932160 | tf_op jit(solution)/shard_map/psum | solution.py:190
  706.7 10.9 %pad_maximum_fusion = bf16[16,448,1280]{2,1,0:T(8,128)(2,1)} fusion(bf16[16,160,1280]{2,1,0:T(8,128)(2,1)} %convolution_convert_fusion.1, bf16[16,288,1280]{2,1,0:T(8,128)(2,1)S(1)} %fusion), kind=kLoop, calls=%fused_computation.16 | loop fusion | flops 36700160 | bytes 36700160 | tf_op jit(solution)/shard_map/concatenate | solution.py:207
  719.6 204.7 %reduce-scatter.5.cloned.1.call-done = bf16[448,1280]{1,0:T(8,128)(2,1)} async-done(((bf16[7168,1280]{1,0:T(8,128)(2,1)}), bf16[448,1280]{1,0:T(8,128)(2,1)}) %reduce-scatter.5.cloned.1.call-update) | async-done | bytes 1146896 | tf_op jit(solution)/shard_map/reduce_scatter | solution.py:206
  (120 shorter events, 148.9 us)
Async XLA Ops:
  7.2 101.4 %all-gather.4.cloned.1.call-start = ((), (), s32[]{:S(2)}) async-start(), calls=%async_computation.6 | async-start | bytes 12533760 | tf_op jit(solution)/shard_map/all_gather | solution.py:141
  7.9 133.9 %reduce-scatter.3.cloned.1.call-start = ((), (), s32[]{:S(2)}) async-start(), calls=%async_computation.7 | async-start | bytes 1966080 | tf_op jit(solution)/shard_map/reduce_scatter | solution.py:152
  115.0 5.1 copy-start.18
  115.0 8.1 copy-start.17
  120.1 159.4 %all-gather.6.cloned.1.call-start = ((), (), s32[]{:S(2)}) async-start(), calls=%async_computation.8 | async-start | bytes 7372800 | tf_op jit(solution)/shard_map/all_gather | solution.py:167
  229.2 92.7 %all-to-all-start.2 = ((bf16[16,4,15,1280]{3,1,2,0:T(4,128)(2,1)}), bf16[16,4,15,1280]{3,1,2,0:T(4,128)(2,1)S(1)}, u32[]{:S(2)}, u32[]{:S(2)}) async-start(bf16[16,4,15,1280]{3,1,2,0:T(4,128)(2,1)} %copy.68), calls=%async_computation.3 | async-start | bytes 4915200 | tf_op jit(solution)/shard_map/all_to_all | solution.py:162
  279.5 12.8 %copy-start.19 = (bf16[1,4,240,2560]{3,2,1,0:T(8,128)(2,1)S(1)}, bf16[1,4,240,2560]{3,2,1,0:T(8,128)(2,1)}, u32[]{:S(2)}) copy-start(bf16[1,4,240,2560]{3,2,1,0:T(8,128)(2,1)} %all-gather.6.cloned.1.call-done) | copy-start | bytes 14745604
  299.8 13.7 %copy-start.2 = (f32[4,240,768]{2,1,0:T(8,128)}, f32[4,240,768]{2,1,0:T(8,128)S(1)}, u32[]{:S(2)}) copy-start(f32[4,240,768]{2,1,0:T(8,128)S(1)} %fusion.5) | copy-start | bytes 8847364
  321.9 134.5 %all-to-all-start.1 = ((bf16[1,4,240,2560]{3,1,0,2:T(4,128)(2,1)}), bf16[1,4,240,2560]{3,1,0,2:T(4,128)(2,1)}, u32[]{:S(2)}, u32[]{:S(2)}) async-start(bf16[1,4,240,2560]{3,1,0,2:T(4,128)(2,1)} %copy.65), calls=%async_computation.2 | async-start | bytes 9830400 | tf_op jit(solution)/shard_map/all_to_all | solution.py:179
  327.6 79.9 %all-gather.8.cloned.1.call-start = ((), (), s32[]{:S(2)}) async-start(), calls=%async_computation.9 | async-start | bytes 7372800 | tf_op jit(solution)/shard_map/all_gather | solution.py:168
  456.4 5.9 copy-start
  456.4 95.9 %all-to-all-start.3 = ((bf16[1,4,240,2560]{3,1,0,2:T(4,128)(2,1)}), bf16[1,4,240,2560]{3,1,0,2:T(4,128)(2,1)}, u32[]{:S(2)}, u32[]{:S(2)}) async-start(bf16[1,4,240,2560]{3,1,0,2:T(4,128)(2,1)} %copy.70), calls=%async_computation.4 | async-start | bytes 9830400 | tf_op jit(solution)/shard_map/all_to_all | solution.py:180
  462.2 462.1 %reduce-scatter.5.cloned.1.call-start = ((), (), s32[]{:S(2)}) async-start(), calls=%async_computation.10 | async-start | bytes 19496960 | tf_op jit(solution)/shard_map/reduce_scatter | solution.py:206
  621.4 2.7 copy-start.10
  621.4 2.8 copy-start.4
  621.4 2.9 copy-start.5
  621.4 2.9 copy-start.6
  621.4 2.9 copy-start.7
  621.4 2.9 copy-start.8
  621.4 3.0 copy-start.9
  698.6 4.6 copy-start.1
  717.7 208.1 %copy-start.3 = (bf16[288,1280]{1,0:T(8,128)(2,1)S(1)}, bf16[288,1280]{1,0:T(8,128)(2,1)}, u32[]{:S(2)}) copy-start(bf16[288,1280]{1,0:T(8,128)(2,1)} %param.14) | copy-start | bytes 2211844
  717.7 208.1 %copy-start.11 = (f32[288,1280]{1,0:T(8,128)S(1)}, f32[288,1280]{1,0:T(8,128)}, u32[]{:S(2)}) copy-start(f32[288,1280]{1,0:T(8,128)} %param.22) | copy-start | bytes 4423684
  925.9 2.6 copy-start.14
  (4 other events, 7.3 us)
Sparse Core Ops, SparseCore 0:
  10.3 98.3 all-gather.3
  120.2 21.5 reduce-scatter.2
  215.7 63.7 all-gather.5
  342.3 65.1 all-gather.7
  717.8 206.3 reduce-scatter.4
where the time goes:
time: 940 us; the launch traced here: 937 us
  waiting for transfers between devices  493 us (52%)
  local copies, waits for them, and re-layouts  147 us (16%)
  blocking collectives  127 us (14%)
  matrix products  99.2 us (11%)
  starting transfers between devices  29.4 us (3%)
  other arithmetic  27.3 us (3%)
  between operations  14.5 us (2%)
    reduce_scatter x1, waiting for transfers between devices, local(): lax.psum_scatter(jnp.concatenate([term_in, term_out], axis=1).reshape(sha...  205 us
    all_gather x1, waiting for transfers between devices, local(): lax.all_gather(proj_in, 'dp', axis=0, tiled=True)  101 us
    psum x1, blocking collectives, local(): total_out, total_in = lax.psum((out_terms, grad_terms_sum), 'mp')  66.1 us
    all_to_all x1, waiting for transfers between devices, local(): lax.all_to_all(input_part.reshape(back_shape), 'dp', split_axis=2, concat...  65.5 us
    all_gather x1, waiting for transfers between devices, local(): lax.all_gather(narrow_grads, 'mp', axis=3, tiled=True)  65.3 us
    gather x12, local copies, waits for them, and re-layouts, collect_rows(): picked = flat[pair_slots[:, choice_index]].astype(jnp.float32)  64.4 us
    all_to_all x1, blocking collectives, local(): lax.all_to_all(send_rows.reshape(send_shape), 'dp', split_axis=0, concat_...  61 us
    all_gather x1, waiting for transfers between devices, local(): lax.all_gather(narrow_rows, 'mp', axis=3, tiled=True)  45.3 us
  transfers between devices with their start and end apart: 8, of which 6 were waited for; matrix products, arithmetic and copies ran while one was open for 15% of the time, Pallas kernels for 0%

commit v1 on v0

v1 whole, which is shorter than its diff:
```python
import jax
import jax.numpy as jnp
from jax import lax
from jax.sharding import PartitionSpec as P

EXPERTS = 64
TOP = 6
CAP = 15


BETA_ONE = 0.9
BETA_TWO = 0.999
EPSILON = 1e-08
LEARN_RATE = 0.001
WEIGHT_DECAY = 0.1
FIRST_FIX = 1.0 - 0.9**50 * 0.9**50
SECOND_FIX = 1.0 - 0.999**50 * 0.999**50


def gelu_parts(preact):

    def smooth(values):
        return jax.nn.gelu(values, approximate=True)

    result, pullback = jax.vjp(smooth, preact)
    return (result, pullback(jnp.ones_like(preact))[0])


def dispatch_masks(routes, gate_weights, slots):
    rows = routes.shape[0]
    expert_ids = jnp.arange(EXPERTS, dtype=jnp.int32)
    hits = routes.T[:, None, :] == expert_ids[None, :, None]
    named = jnp.any(hits, axis=0)
    weight = jnp.sum(jnp.where(hits, gate_weights.T[:, None, :], 0.0), axis=0)
    before = (jnp.arange(rows)[:, None] < jnp.arange(rows)[None, :]).astype(jnp.bfloat16)
    earlier = jnp.dot(named.astype(jnp.bfloat16), before, preferred_element_type=jnp.float32)
    slot_of = jnp.where(named, earlier.astype(jnp.int32), -1)
    place = slot_of[:, None, :] == jnp.arange(slots, dtype=jnp.int32)[None, :, None]
    weighted = jnp.where(place, weight[:, None, :], 0.0)
    return (
        place.astype(jnp.bfloat16).reshape(EXPERTS * slots, rows),
        weighted.reshape(EXPERTS * slots, rows),
    )


def adamw_update(weight, gradient, first, second):
    first_new = BETA_ONE * first + (1.0 - BETA_ONE) * gradient
    second_new = BETA_TWO * second + (1.0 - BETA_TWO) * gradient * gradient
    update = first_new / FIRST_FIX / (jnp.sqrt(second_new / SECOND_FIX) + EPSILON)
    current = weight.astype(jnp.float32)
    return (
        (current - LEARN_RATE * (update + WEIGHT_DECAY * current)).astype(jnp.bfloat16),
        first_new,
        second_new,
    )


def rows_dot(table, rows):
    return lax.dot_general(
        table, rows, (((0,), (0,)), ((), ())), preferred_element_type=jnp.float32
    )


def local(
    features,
    proj_in,
    proj_out,
    expert_gate,
    expert_up,
    expert_down,
    routes,
    gate_weights,
    cotangent,
    first_in,
    second_in,
    first_out,
    second_out,
):
    row_count = features.shape[0]
    model_width = cotangent.shape[1]
    data_parts = lax.axis_size("dp")
    model_parts = lax.axis_size("mp")
    data_place = lax.axis_index("dp")
    model_place = lax.axis_index("mp")
    column_width = model_width // model_parts
    column_start = model_place * column_width
    own_experts = expert_gate.shape[0]
    slots = -(-CAP // 16) * 16
    expert_rows = data_parts * slots
    width_part = model_width // data_parts

    def exchange(rows):
        blocks = lax.all_to_all(
            rows.reshape(data_parts, own_experts, slots, rows.shape[-1]),
            "dp",
            split_axis=0,
            concat_axis=0,
            tiled=True,
        )
        return blocks.transpose(1, 0, 2, 3).reshape(own_experts, expert_rows, rows.shape[-1])

    def widen(rows):
        return lax.all_gather(rows, "mp", axis=rows.ndim - 1, tiled=True)

    def columns_of(rows):
        return lax.all_to_all(rows, "dp", split_axis=1, concat_axis=0, tiled=True)

    proj_full = lax.all_gather(proj_in, "dp", axis=0, tiled=True)
    place, weighted = dispatch_masks(routes, gate_weights, slots)
    slot_weight = jnp.sum(weighted, axis=1, keepdims=True)
    cotangent_cols = lax.dynamic_slice_in_dim(cotangent, column_start, column_width, 1)
    send_grads = (
        slot_weight * jnp.dot(place, cotangent_cols, preferred_element_type=jnp.float32)
    ).astype(jnp.bfloat16)
    narrow_grads = exchange(send_grads)
    feature_cols = columns_of(features)
    proj_full, narrow_grads, feature_cols = lax.optimization_barrier(
        (proj_full, narrow_grads, feature_cols)
    )

    preact = jnp.dot(features, proj_full, preferred_element_type=jnp.float32)
    activated, gelu_slope = gelu_parts(preact)
    hidden = activated.astype(jnp.bfloat16)
    partial_value = jnp.dot(hidden, proj_out, preferred_element_type=jnp.float32)
    mapped_cols = lax.psum_scatter(partial_value, "mp", scatter_dimension=1, tiled=True).astype(
        jnp.bfloat16
    )
    mapped_cols, narrow_grads = lax.optimization_barrier((mapped_cols, narrow_grads))
    grads_in = widen(narrow_grads)
    send_rows = jnp.dot(place, mapped_cols, preferred_element_type=jnp.float32).astype(
        jnp.bfloat16
    )
    inputs = widen(exchange(send_rows))
    inputs, hidden_sent = lax.optimization_barrier((inputs, hidden))
    hidden_all = lax.all_gather(hidden_sent, "dp", axis=0, tiled=True)

    down_gradient = jnp.einsum(
        "erd,efd->erf", grads_in, expert_down, preferred_element_type=jnp.float32
    )
    gate_value = jnp.einsum("erd,edf->erf", inputs, expert_gate, preferred_element_type=jnp.float32)
    up_value = jnp.einsum("erd,edf->erf", inputs, expert_up, preferred_element_type=jnp.float32)
    sigmoid_gate = jax.nn.sigmoid(gate_value)
    silu_gate = gate_value * sigmoid_gate
    inner = (silu_gate * up_value).astype(jnp.bfloat16)
    gate_gradient = (
        down_gradient * up_value * sigmoid_gate * (1.0 + gate_value * (1.0 - sigmoid_gate))
    ).astype(jnp.bfloat16)
    up_gradient = (down_gradient * silu_gate).astype(jnp.bfloat16)
    input_part = (
        jnp.einsum("erf,edf->erd", gate_gradient, expert_gate, preferred_element_type=jnp.float32)
        + jnp.einsum("erf,edf->erd", up_gradient, expert_up, preferred_element_type=jnp.float32)
    ).astype(jnp.bfloat16)
    inner, input_part = lax.optimization_barrier((inner, input_part))
    out_part = jnp.einsum(
        "erf,efd->erd", inner, expert_down, preferred_element_type=jnp.float32
    ).astype(jnp.bfloat16)

    def narrow(part):
        return lax.psum_scatter(part, "mp", scatter_dimension=2, tiled=True)

    def send_back(part):
        blocks = part.reshape(own_experts, data_parts, slots, column_width)
        return lax.all_to_all(
            blocks.transpose(1, 0, 2, 3), "dp", split_axis=0, concat_axis=0, tiled=True
        ).reshape(EXPERTS * slots, column_width)

    narrow_in = narrow(input_part)
    out_part, narrow_in = lax.optimization_barrier((out_part, narrow_in))
    narrow_out = narrow(out_part)
    back_in = send_back(narrow_in)
    grad_cols = (
        cotangent_cols.astype(jnp.float32) + rows_dot(place, back_in)
    ).astype(jnp.bfloat16)
    grad_mapped = widen(grad_cols)
    grad_hidden = lax.dot_general(
        grad_mapped, proj_out, (((1,), (1,)), ((), ())), preferred_element_type=jnp.float32
    )
    grad_pre = (grad_hidden * gelu_slope).astype(jnp.bfloat16)
    grad_pre, grad_mapped, narrow_out = lax.optimization_barrier(
        (grad_pre, grad_mapped, narrow_out)
    )
    grad_pre_all = lax.all_gather(grad_pre, "dp", axis=0, tiled=True)
    mapped_grad_cols = columns_of(grad_mapped)
    back_out = send_back(narrow_out)
    weight_high = weighted.astype(jnp.bfloat16)
    weight_low = (weighted - weight_high.astype(jnp.float32)).astype(jnp.bfloat16)
    out_cols = (
        mapped_cols.astype(jnp.float32)
        + rows_dot(weight_high, back_out)
        + rows_dot(weight_low, back_out)
    ).astype(jnp.bfloat16)
    moe_out = widen(out_cols)
    grad_out = rows_dot(hidden_all, mapped_grad_cols)
    grad_in = rows_dot(feature_cols, grad_pre_all)
    own_out = lax.dynamic_slice_in_dim(proj_out, data_place * width_part, width_part, 1)
    new_in, first_in_new, second_in_new = adamw_update(proj_in, grad_in, first_in, second_in)
    new_out, first_out_new, second_out_new = adamw_update(own_out, grad_out, first_out, second_out)
    return (moe_out, new_in, new_out, first_in_new, second_in_new, first_out_new, second_out_new)


def solution(mesh):
    return jax.shard_map(
        local,
        mesh=mesh,
        in_specs=(
            P("dp", None),
            P("dp", "mp"),
            P("mp", None),
            P("dp", None, "mp"),
            P("dp", None, "mp"),
            P("dp", "mp", None),
            P("dp", None),
            P("dp", None),
            P("dp", None),
            P("dp", "mp"),
            P("dp", "mp"),
            P("mp", "dp"),
            P("mp", "dp"),
        ),
        out_specs=(
            P("dp", None),
            P("dp", "mp"),
            P("mp", "dp"),
            P("dp", "mp"),
            P("dp", "mp"),
            P("mp", "dp"),
            P("mp", "dp"),
        ),
        check_vma=False,
    )
```

time: 940 us -> 723 us (0.77)
  local copies, waits for them, and re-layouts: 147 us -> 22.6 us
  waiting for transfers between devices: 493 us -> 428 us
  blocking collectives: 127 us -> 86.6 us
  other arithmetic: 27.3 us -> 2.32 us
  starting transfers between devices: 29.4 us -> 52.1 us
  matrix products: 99.2 us -> 117 us
    all_to_all x3 -> x5, waiting for transfers between devices: 65.5 us -> 223 us  [the longest x1 87.7 us: exchange(): lax.all_to_all(rows.reshape(data_parts, own_experts, slots, rows.shape[-1...]
    reduce_scatter x1 -> x2, waiting for transfers between devices: 205 us -> 54.2 us  [narrow(): return lax.psum_scatter(part, 'mp', scatter_dimension=2, tiled=True)]
    all_gather x3 -> x5, waiting for transfers between devices: 211 us -> 124 us  [the longest x2 59.3 us: widen(): return lax.all_gather(rows, 'mp', axis=rows.ndim - 1, tiled=True)]
    gather x16 -> x0, local copies, waits for them, and re-layouts: 81.3 us -> none  [the longest x12 64.4 us: collect_rows(): picked = flat[pair_slots[:, choice_index]].astype(jnp.float32)]
    psum x1 -> x0, blocking collectives: 66.1 us -> none  [local(): total_out, total_in = lax.psum((out_terms, grad_terms_sum), 'mp')]
    all_to_all x3 -> x5, starting transfers between devices: 16.5 us -> 51.3 us  [the longest x2 19 us: columns_of(): return lax.all_to_all(rows, 'dp', split_axis=1, concat_axis=0, tiled=True)]
    reshape x5 -> x2, local copies, waits for them, and re-layouts: 32.6 us -> 3.63 us  [send_back(): blocks = part.reshape(own_experts, data_parts, slots, column_width)]
    all_gather x0 -> x2, blocking collectives: none -> 22.8 us  [widen(): return lax.all_gather(rows, 'mp', axis=rows.ndim - 1, tiled=True)]
  transfers between devices with their start and end apart: 8 -> 13, of which waited for: 6 -> 12; matrix products, arithmetic and copies ran while one was open for 15% -> 9% of each run, Pallas kernels for 0% -> 0%
where the time goes in v1:
time: 723 us; the launch traced here: 722 us
  waiting for transfers between devices  428 us (59%)
  matrix products  117 us (16%)
  blocking collectives  86.6 us (12%)
  starting transfers between devices  52.1 us (7%)
  local copies, waits for them, and re-layouts  22.6 us (3%)
  between operations  14.4 us (2%)
    all_to_all x1, waiting for transfers between devices, exchange(): lax.all_to_all(rows.reshape(data_parts, own_experts, slots, rows.shape[-1...  87.7 us
    all_to_all x2, waiting for transfers between devices, send_back(): lax.all_to_all(blocks.transpose(1, 0, 2, 3), 'dp', split_axis=0, concat_a...  79.4 us
    all_to_all x1, blocking collectives, exchange(): lax.all_to_all(rows.reshape(data_parts, own_experts, slots, rows.shape[-1...  63.8 us
    all_gather x2, waiting for transfers between devices, widen(): return lax.all_gather(rows, 'mp', axis=rows.ndim - 1, tiled=True)  59.3 us
    all_to_all x2, waiting for transfers between devices, columns_of(): return lax.all_to_all(rows, 'dp', split_axis=1, concat_axis=0, tiled=True)  55.6 us
    reduce_scatter x2, waiting for transfers between devices, narrow(): return lax.psum_scatter(part, 'mp', scatter_dimension=2, tiled=True)  54.2 us
    reduce_scatter x1, waiting for transfers between devices, local(): lax.psum_scatter(partial_value, 'mp', scatter_dimension=1, tiled=True)  25.9 us
    all_gather x1, waiting for transfers between devices, local(): grad_pre_all = lax.all_gather(grad_pre, 'dp', axis=0, tiled=True)  25.9 us
  transfers between devices with their start and end apart: 13, of which 12 were waited for; matrix products, arithmetic and copies ran while one was open for 9% of the time, Pallas kernels for 0%

profile of v1, /device:TPU:0, one launch (start us, length us, event | category | flops | bytes accessed | tf_op | source)
XLA Modules:
  0.0 722.4 jit_solution(11303930736655657197)
XLA Ops:
  21.5 37.2 %all-to-all-done.1 = bf16[128,16,288]{0,2,1:T(8,128)(2,1)S(1)} async-done(((bf16[128,16,288]{0,2,1:T(8,128)(2,1)}), bf16[128,16,288]{0,2,1:T(8,128)(2,1)S(1)}, u32[]{:S(2)}, u32[]{:S(2)}) %all-to-all-start.1) | async-done | bytes 1179680 | tf_op jit(solution)/shard_map/all_to_all | solution.py:106
  59.8 14.5 %all-to-all-start = ((bf16[16,4,16,1280]{3,2,1,0:T(8,128)(2,1)}), bf16[16,4,16,1280]{3,2,1,0:T(8,128)(2,1)S(1)}, u32[]{:S(2)}, u32[]{:S(2)}) async-start(bf16[16,4,16,1280]{3,2,1,0:T(8,128)(2,1)} %bitcast.3), calls=%async_computation | async-start | bytes 5242880 | tf_op jit(solution)/shard_map/all_to_all | solution.py:93
  76.8 87.7 %all-to-all-done = bf16[16,4,16,1280]{3,2,1,0:T(8,128)(2,1)S(1)} async-done(((bf16[16,4,16,1280]{3,2,1,0:T(8,128)(2,1)}), bf16[16,4,16,1280]{3,2,1,0:T(8,128)(2,1)S(1)}, u32[]{:S(2)}, u32[]{:S(2)}) %all-to-all-start) | async-done | bytes 2621472 | tf_op jit(solution)/shard_map/all_to_all | solution.py:93
  166.2 13.7 %all-gather.6.cloned.1.call-done = bf16[4608,1280]{1,0:T(8,128)(2,1)} async-done(((bf16[288,1280]{1,0:T(8,128)(2,1)}), bf16[4608,1280]{1,0:T(8,128)(2,1)}) %all-gather.6.cloned.1.call-update) | async-done | bytes 11796496 | tf_op jit(solution)/shard_map/all_gather | solution.py:108
  179.9 8.7 %multiply_convert_fusion.6 = (bf16[128,1280]{0,1:T(8,128)(2,1)S(1)}, f32[128,1280]{0,1:T(8,128)}) fusion(bf16[4608,1280]{1,0:T(8,128)(2,1)} %all-gather.6.cloned.1.call-done, bf16[128,4608]{1,0:T(8,128)(2,1)} %param.13), kind=kOutput, calls=%fused_computation.54 | convolution fusion | flops 1511424000 | bytes 13959168 | tf_op jit(solution)/shard_map/dot_general | solution.py:121
  193.8 25.9 %reduce-scatter.4.cloned.1.call-done = f32[128,1280]{1,0:T(8,128)} async-done(((f32[128,2560]{1,0:T(8,128)}), f32[128,1280]{1,0:T(8,128)}) %reduce-scatter.4.cloned.1.call-update) | async-done | bytes 655376 | tf_op jit(solution)/shard_map/reduce_scatter | solution.py:125
  221.7 63.8 %all_to_all.58 = bf16[16,4,16,1280]{3,2,1,0:T(8,128)(2,1)S(1)} all-to-all(bf16[16,4,16,1280]{3,2,1,0:T(8,128)(2,1)S(1)} %bitcast.80), channel_id=1, replica_groups=mesh['dp'=16,'mp'=2] {'dp'}, dimensions={0} | all-to-all | bytes 5242880 | tf_op jit(solution)/shard_map/all_to_all | solution.py:93
  289.8 13.0 %fusion.35 = f32[4,256,768]{2,1,0:T(8,128)} fusion(bf16[4,256,2560]{2,1,0:T(8,128)(2,1)} %all-gather.10.cloned.1.call-done, bf16[4,768,2560]{2,1,0:T(8,128)(2,1)} %param.18), kind=kOutput, calls=%fused_computation.69 | convolution fusion | flops 4026531840 | bytes 24117248 | tf_op jit(solution)/shard_map/erd,efd->erf/dot_general | solution.py:137
  302.8 57.0 %all-gather.8.cloned.1.call-done = bf16[4,256,2560]{2,1,0:T(8,128)(2,1)} async-done(((bf16[4,256,1280]{2,1,0:T(8,128)(2,1)}), bf16[4,256,2560]{2,1,0:T(8,128)(2,1)}) %all-gather.8.cloned.1.call-update) | async-done | bytes 5242896 | tf_op jit(solution)/shard_map/all_gather | solution.py:103
  359.8 10.1 %fusion.34 = f32[4,256,768]{2,1,0:T(8,128)S(1)} fusion(bf16[4,256,2560]{2,1,0:T(8,128)(2,1)} %all-gather.8.cloned.1.call-done, bf16[4,2560,768]{2,1,0:T(8,128)(2,1)} %param.16), kind=kOutput, calls=%fused_computation.68 | convolution fusion | flops 4026531840 | bytes 24117248 | tf_op jit(solution)/shard_map/erd,edf->erf/dot_general | solution.py:140
  369.9 12.8 %multiply_convert_fusion.3 = (bf16[4,256,768]{2,1,0:T(8,128)(2,1)S(1)}, f32[4,256,768]{2,1,0:T(8,128)}) fusion(f32[4,256,768]{2,1,0:T(8,128)S(1)} %fusion.34, bf16[4,256,2560]{2,1,0:T(8,128)(2,1)S(1)} %copy-done.9, bf16[4,2560,768]{2,1,0:T(8,128)(2,1)} %param.17), kind=kOutput, calls=%fused_computation.6 | convolution fusion | flops 4031250432 | bytes 28835840 | tf_op jit(solution)/shard_map/erd,edf->erf/dot_general | solution.py:141
  382.7 13.3 %fusion.4 = f32[4,256,2560]{2,1,0:T(8,128)} fusion(bf16[4,2560,768]{2,1,0:T(8,128)(2,1)} %param.16, f32[4,256,768]{2,1,0:T(8,128)} %copy-done.10, f32[4,256,768]{2,1,0:T(8,128)} %fusion.35, f32[4,256,768]{2,1,0:T(8,128)} %get-tuple-element.46), kind=kOutput, calls=%fused_computation.22 | convolution fusion | flops 4034396160 | bytes 35651584 | tf_op jit(solution)/shard_map/erf,edf->erd/dot_general | solution.py:150
  396.0 15.0 %add_convert_fusion = bf16[4,256,2560]{2,1,0:T(8,128)(2,1)} fusion(f32[4,256,2560]{2,1,0:T(8,128)} %fusion.4, bf16[4,2560,768]{2,1,0:T(8,128)(2,1)} %param.17, f32[4,256,768]{2,1,0:T(8,128)} %fusion.35, f32[4,256,768]{2,1,0:T(8,128)} %copy-done.10), kind=kOutput, calls=%fused_computation | convolution fusion | flops 4036493312 | bytes 37748736 | tf_op jit(solution)/shard_map/erf,edf->erd/dot_general | solution.py:151
  411.3 11.5 %convolution_convert_fusion = bf16[4,256,2560]{2,1,0:T(8,128)(2,1)} fusion(bf16[4,256,768]{2,1,0:T(8,128)(2,1)S(1)} %get-tuple-element.26, bf16[4,768,2560]{2,1,0:T(8,128)(2,1)} %param.18), kind=kOutput, calls=%fused_computation.1 | convolution fusion | flops 4029153280 | bytes 22544384 | tf_op jit(solution)/shard_map/erf,efd->erd/dot_general | solution.py:154
  422.8 54.2 %reduce-scatter.6.cloned.1.call-done = bf16[4,256,1280]{2,1,0:T(8,128)(2,1)} async-done(((bf16[4,256,2560]{2,1,0:T(8,128)(2,1)}), bf16[4,256,1280]{2,1,0:T(8,128)(2,1)}) %reduce-scatter.6.cloned.1.call-update) | async-done | bytes 2621456 | tf_op jit(solution)/shard_map/reduce_scatter | solution.py:159
  486.3 50.0 %all-to-all-done.3 = bf16[16,4,16,1280]{3,2,1,0:T(8,128)(2,1)S(1)} async-done(((bf16[16,4,16,1280]{3,2,1,0:T(8,128)(2,1)}), bf16[16,4,16,1280]{3,2,1,0:T(8,128)(2,1)S(1)}, u32[]{:S(2)}, u32[]{:S(2)}) %all-to-all-start.3) | async-done | bytes 2621472 | tf_op jit(solution)/shard_map/all_to_all | solution.py:163
  537.8 12.5 %all_gather.24 = bf16[128,2560]{1,0:T(8,128)(2,1)S(1)} all-gather(bf16[128,1280]{1,0:T(8,128)(2,1)S(1)} %fusion.1), channel_id=1, replica_groups=mesh['dp'=16,'mp'=2] {'mp'}, dimensions={1}, use_global_device_ids=true | all-gather | bytes 983040 | tf_op jit(solution)/shard_map/all_gather | solution.py:103
  559.0 11.6 %all-to-all-start.5 = ((bf16[128,16,160]{0,2,1:T(8,128)(2,1)}), bf16[128,16,160]{0,2,1:T(8,128)(2,1)}, u32[]{:S(2)}, u32[]{:S(2)}) async-start(bf16[128,16,160]{0,2,1:T(8,128)(2,1)} %bitcast.84), calls=%async_computation.8 | async-start | bytes 1310720 | tf_op jit(solution)/shard_map/all_to_all | solution.py:106
  572.5 18.4 %all-to-all-done.5 = bf16[128,16,160]{0,2,1:T(8,128)(2,1)} async-done(((bf16[128,16,160]{0,2,1:T(8,128)(2,1)}), bf16[128,16,160]{0,2,1:T(8,128)(2,1)}, u32[]{:S(2)}, u32[]{:S(2)}) %all-to-all-start.5) | async-done | bytes 655392 | tf_op jit(solution)/shard_map/all_to_all | solution.py:106
  590.9 12.2 %all-to-all-start.4 = ((bf16[16,4,16,1280]{3,2,1,0:T(8,128)(2,1)}), bf16[16,4,16,1280]{3,2,1,0:T(8,128)(2,1)S(1)}, u32[]{:S(2)}, u32[]{:S(2)}) async-start(bf16[16,4,16,1280]{3,2,1,0:T(8,128)(2,1)} %bitcast.75), calls=%async_computation.7 | async-start | bytes 5242880 | tf_op jit(solution)/shard_map/all_to_all | solution.py:163
  607.6 24.8 %all-gather.14.cloned.1.call-done = bf16[2048,1280]{0,1:T(8,128)(2,1)} async-done(((bf16[128,1280]{0,1:T(8,128)(2,1)}), bf16[2048,1280]{0,1:T(8,128)(2,1)}) %all-gather.14.cloned.1.call-update) | async-done | bytes 5242896 | tf_op jit(solution)/shard_map/all_gather | solution.py:135
  639.4 29.4 %all-to-all-done.4 = bf16[16,4,16,1280]{3,2,1,0:T(8,128)(2,1)S(1)} async-done(((bf16[16,4,16,1280]{3,2,1,0:T(8,128)(2,1)}), bf16[16,4,16,1280]{3,2,1,0:T(8,128)(2,1)S(1)}, u32[]{:S(2)}, u32[]{:S(2)}) %all-to-all-start.4) | async-done | bytes 2621472 | tf_op jit(solution)/shard_map/all_to_all | solution.py:163
  669.9 10.4 %all_gather.25 = bf16[128,2560]{1,0:T(8,128)(2,1)S(1)} all-gather(bf16[128,1280]{1,0:T(8,128)(2,1)S(1)} %fusion.3), channel_id=1, replica_groups=mesh['dp'=16,'mp'=2] {'mp'}, dimensions={1}, use_global_device_ids=true | all-gather | bytes 983040 | tf_op jit(solution)/shard_map/all_gather | solution.py:103
  680.3 25.9 %all-gather.12.cloned.1.call-done = bf16[2048,1280]{0,1:T(8,128)(2,1)} async-done(((bf16[128,1280]{0,1:T(8,128)(2,1)}), bf16[2048,1280]{0,1:T(8,128)(2,1)}) %all-gather.12.cloned.1.call-update) | async-done | bytes 5242896 | tf_op jit(solution)/shard_map/all_gather | solution.py:182
  (74 shorter events, 74.6 us)
Async XLA Ops:
  7.2 10.6 %copy-start.7 = (s32[128,6]{0,1:T(8,128)S(1)}, s32[128,6]{0,1:T(8,128)}, u32[]{:S(2)}) copy-start(s32[128,6]{0,1:T(8,128)} %param.19) | copy-start | bytes 9220
  7.2 10.6 %copy-start.8 = (f32[128,6]{0,1:T(8,128)S(1)}, f32[128,6]{0,1:T(8,128)}, u32[]{:S(2)}) copy-start(f32[128,6]{0,1:T(8,128)} %param.20) | copy-start | bytes 9220
  7.2 11.9 %copy-start.6 = (bf16[128,2560]{1,0:T(8,128)(2,1)S(1)}, bf16[128,2560]{1,0:T(8,128)(2,1)}, u32[]{:S(2)}) copy-start(bf16[128,2560]{1,0:T(8,128)(2,1)} %param.21) | copy-start | bytes 1966084
  7.2 172.7 %all-gather.6.cloned.1.call-start = ((), (), s32[]{:S(2)}) async-start(), calls=%async_computation.9 | async-start | bytes 12533760 | tf_op jit(solution)/shard_map/all_gather | solution.py:108
  10.3 48.4 %all-to-all-start.1 = ((bf16[128,16,288]{0,2,1:T(8,128)(2,1)}), bf16[128,16,288]{0,2,1:T(8,128)(2,1)S(1)}, u32[]{:S(2)}, u32[]{:S(2)}) async-start(bf16[128,16,288]{0,2,1:T(8,128)(2,1)} %bitcast.6), calls=%async_computation.1 | async-start | bytes 2359296 | tf_op jit(solution)/shard_map/all_to_all | solution.py:106
  58.7 1.0 copy-start
  59.8 104.7 %all-to-all-start = ((bf16[16,4,16,1280]{3,2,1,0:T(8,128)(2,1)}), bf16[16,4,16,1280]{3,2,1,0:T(8,128)(2,1)S(1)}, u32[]{:S(2)}, u32[]{:S(2)}) async-start(bf16[16,4,16,1280]{3,2,1,0:T(8,128)(2,1)} %bitcast.3), calls=%async_computation | async-start | bytes 5242880 | tf_op jit(solution)/shard_map/all_to_all | solution.py:93
  74.2 145.5 %reduce-scatter.4.cloned.1.call-start = ((), (), s32[]{:S(2)}) async-start(), calls=%async_computation.10 | async-start | bytes 1966080 | tf_op jit(solution)/shard_map/reduce_scatter | solution.py:125
  188.6 5.1 copy-start.4
  193.7 96.1 %all-gather.10.cloned.1.call-start = ((), (), s32[]{:S(2)}) async-start(), calls=%async_computation.12 | async-start | bytes 7864320 | tf_op jit(solution)/shard_map/all_gather | solution.py:103
  220.9 138.9 %all-gather.8.cloned.1.call-start = ((), (), s32[]{:S(2)}) async-start(), calls=%async_computation.11 | async-start | bytes 7864320 | tf_op jit(solution)/shard_map/all_gather | solution.py:103
  287.3 189.7 %reduce-scatter.6.cloned.1.call-start = ((), (), s32[]{:S(2)}) async-start(), calls=%async_computation.13 | async-start | bytes 7864320 | tf_op jit(solution)/shard_map/reduce_scatter | solution.py:159
  359.8 10.1 %copy-start.9 = (bf16[4,256,2560]{2,1,0:T(8,128)(2,1)S(1)}, bf16[4,256,2560]{2,1,0:T(8,128)(2,1)}, u32[]{:S(2)}) copy-start(bf16[4,256,2560]{2,1,0:T(8,128)(2,1)} %all-gather.8.cloned.1.call-done) | copy-start | bytes 15728644
  369.9 12.8 %copy-start.10 = (f32[4,256,768]{2,1,0:T(8,128)}, f32[4,256,768]{2,1,0:T(8,128)S(1)}, u32[]{:S(2)}) copy-start(f32[4,256,768]{2,1,0:T(8,128)S(1)} %fusion.34) | copy-start | bytes 9437188
  411.1 145.6 %reduce-scatter.8.cloned.1.call-start = ((), (), s32[]{:S(2)}) async-start(), calls=%async_computation.14 | async-start | bytes 7864320 | tf_op jit(solution)/shard_map/reduce_scatter | solution.py:159
  477.0 1.7 copy-start.2
  477.0 155.4 %all-gather.14.cloned.1.call-start = ((), (), s32[]{:S(2)}) async-start(), calls=%async_computation.16 | async-start | bytes 5570560 | tf_op jit(solution)/shard_map/all_gather | solution.py:135
  480.5 55.7 %all-to-all-start.3 = ((bf16[16,4,16,1280]{3,2,1,0:T(8,128)(2,1)}), bf16[16,4,16,1280]{3,2,1,0:T(8,128)(2,1)S(1)}, u32[]{:S(2)}, u32[]{:S(2)}) async-start(bf16[16,4,16,1280]{3,2,1,0:T(8,128)(2,1)} %bitcast.79), calls=%async_computation.5 | async-start | bytes 5242880 | tf_op jit(solution)/shard_map/all_to_all | solution.py:163
  486.1 220.0 %all-gather.12.cloned.1.call-start = ((), (), s32[]{:S(2)}) async-start(), calls=%async_computation.15 | async-start | bytes 5570560 | tf_op jit(solution)/shard_map/all_gather | solution.py:182
  536.2 14.9 %copy-start.11 = (f32[128,1280]{0,1:T(8,128)S(1)}, f32[128,1280]{0,1:T(8,128)}, u32[]{:S(2)}) copy-start(f32[128,1280]{0,1:T(8,128)} %get-tuple-element.44) | copy-start | bytes 1966084
  556.7 13.9 %copy-start.1 = (bf16[4,256,1280]{2,1,0:T(8,128)(2,1)S(1)}, bf16[4,256,1280]{2,1,0:T(8,128)(2,1)}, u32[]{:S(2)}) copy-start(bf16[4,256,1280]{2,1,0:T(8,128)(2,1)} %reduce-scatter.8.cloned.1.call-done) | copy-start | bytes 7864324
  559.0 31.9 %all-to-all-start.5 = ((bf16[128,16,160]{0,2,1:T(8,128)(2,1)}), bf16[128,16,160]{0,2,1:T(8,128)(2,1)}, u32[]{:S(2)}, u32[]{:S(2)}) async-start(bf16[128,16,160]{0,2,1:T(8,128)(2,1)} %bitcast.84), calls=%async_computation.8 | async-start | bytes 1310720 | tf_op jit(solution)/shard_map/all_to_all | solution.py:106
  590.9 77.9 %all-to-all-start.4 = ((bf16[16,4,16,1280]{3,2,1,0:T(8,128)(2,1)}), bf16[16,4,16,1280]{3,2,1,0:T(8,128)(2,1)S(1)}, u32[]{:S(2)}, u32[]{:S(2)}) async-start(bf16[16,4,16,1280]{3,2,1,0:T(8,128)(2,1)} %bitcast.75), calls=%async_computation.7 | async-start | bytes 5242880 | tf_op jit(solution)/shard_map/all_to_all | solution.py:163
  639.4 30.0 %copy-start.5 = (bf16[64,16,128]{2,1,0:T(8,128)(2,1)S(1)}, bf16[64,16,128]{2,1,0:T(8,128)(2,1)}, u32[]{:S(2)}) copy-start(bf16[64,16,128]{2,1,0:T(8,128)(2,1)} %get-tuple-element.41) | copy-start | bytes 786436
  (1 other events, 0.8 us)
Sparse Core Ops, SparseCore 0:
  10.3 169.5 all-gather.5
  193.9 25.8 reduce-scatter.3
  221.3 68.5 all-gather.9
  291.2 68.5 all-gather.7
  411.2 65.7 reduce-scatter.5
  479.1 67.1 reduce-scatter.7
  549.1 83.3 all-gather.13
  635.2 70.9 all-gather.11

commit v2 on v1

--- a/solution.py
+++ b/solution.py
@@ -113,10 +113,7 @@
         slot_weight * jnp.dot(place, cotangent_cols, preferred_element_type=jnp.float32)
     ).astype(jnp.bfloat16)
     narrow_grads = exchange(send_grads)
-    feature_cols = columns_of(features)
-    proj_full, narrow_grads, feature_cols = lax.optimization_barrier(
-        (proj_full, narrow_grads, feature_cols)
-    )
+    proj_full, narrow_grads = lax.optimization_barrier((proj_full, narrow_grads))
 
     preact = jnp.dot(features, proj_full, preferred_element_type=jnp.float32)
     activated, gelu_slope = gelu_parts(preact)
@@ -130,8 +127,10 @@
     send_rows = jnp.dot(place, mapped_cols, preferred_element_type=jnp.float32).astype(
         jnp.bfloat16
     )
-    inputs = widen(exchange(send_rows))
-    inputs, hidden_sent = lax.optimization_barrier((inputs, hidden))
+    narrow_rows, features_sent = lax.optimization_barrier((exchange(send_rows), features))
+    inputs = widen(narrow_rows)
+    feature_cols = columns_of(features_sent)
+    inputs, hidden_sent, feature_cols = lax.optimization_barrier((inputs, hidden, feature_cols))
     hidden_all = lax.all_gather(hidden_sent, "dp", axis=0, tiled=True)
 
     down_gradient = jnp.einsum(

time: 723 us -> 693 us (0.959)
  waiting for transfers between devices: 428 us -> 302 us
  blocking collectives: 86.6 us -> 200 us
  starting transfers between devices: 52.1 us -> 35.7 us
    all_to_all x1 -> x2, blocking collectives: 63.8 us -> 177 us  [exchange(): lax.all_to_all(rows.reshape(data_parts, own_experts, slots, rows.shape[-1...]
    all_to_all x1 -> x0, waiting for transfers between devices: 87.7 us -> none  [exchange(): lax.all_to_all(rows.reshape(data_parts, own_experts, slots, rows.shape[-1...]
    all_to_all x2, waiting for transfers between devices: 55.6 us -> 28.5 us  [columns_of(): return lax.all_to_all(rows, 'dp', split_axis=1, concat_axis=0, tiled=True)]
    all_gather x2, waiting for transfers between devices: 59.3 us -> 39.7 us  [widen(): return lax.all_gather(rows, 'mp', axis=rows.ndim - 1, tiled=True)]
    all_to_all x1 -> x0, starting transfers between devices: 14.5 us -> none  [exchange(): lax.all_to_all(rows.reshape(data_parts, own_experts, slots, rows.shape[-1...]
    all_gather x1, waiting for transfers between devices: 13.7 us -> 26 us  [local(): proj_full = lax.all_gather(proj_in, 'dp', axis=0, tiled=True)]
  transfers between devices with their start and end apart: 13 -> 12, of which waited for: 12 -> 10; matrix products, arithmetic and copies ran while one was open for 9% -> 9% of each run, Pallas kernels for 0% -> 0%
where the time goes in v2:
time: 693 us; the launch traced here: 691 us
  waiting for transfers between devices  302 us (44%)
  blocking collectives  200 us (29%)
  matrix products  117 us (17%)
  starting transfers between devices  35.7 us (5%)
  local copies, waits for them, and re-layouts  19.3 us (3%)
  between operations  14.3 us (2%)
    all_to_all x2, blocking collectives, exchange(): lax.all_to_all(rows.reshape(data_parts, own_experts, slots, rows.shape[-1...  177 us
    all_to_all x2, waiting for transfers between devices, send_back(): lax.all_to_all(blocks.transpose(1, 0, 2, 3), 'dp', split_axis=0, concat_a...  79.5 us
    reduce_scatter x2, waiting for transfers between devices, narrow(): return lax.psum_scatter(part, 'mp', scatter_dimension=2, tiled=True)  54.1 us
    all_gather x2, waiting for transfers between devices, widen(): return lax.all_gather(rows, 'mp', axis=rows.ndim - 1, tiled=True)  39.7 us
    all_to_all x2, waiting for transfers between devices, columns_of(): return lax.all_to_all(rows, 'dp', split_axis=1, concat_axis=0, tiled=True)  28.5 us
    all_gather x1, waiting for transfers between devices, local(): proj_full = lax.all_gather(proj_in, 'dp', axis=0, tiled=True)  26 us
    all_gather x1, waiting for transfers between devices, local(): grad_pre_all = lax.all_gather(grad_pre, 'dp', axis=0, tiled=True)  25.7 us
    all_gather x1, waiting for transfers between devices, local(): hidden_all = lax.all_gather(hidden_sent, 'dp', axis=0, tiled=True)  24.7 us
  transfers between devices with their start and end apart: 12, of which 10 were waited for; matrix products, arithmetic and copies ran while one was open for 9% of the time, Pallas kernels for 0%

profile of v2, /device:TPU:0, one launch (start us, length us, event | category | flops | bytes accessed | tf_op | source)
XLA Modules:
  0.0 691.5 jit_solution(2917863131670453128)
XLA Ops:
  12.0 113.0 %all_to_all.58 = bf16[16,4,16,1280]{3,2,1,0:T(8,128)(2,1)S(1)} all-to-all(bf16[16,4,16,1280]{3,2,1,0:T(8,128)(2,1)S(1)} %bitcast.79), channel_id=1, replica_groups=mesh['dp'=16,'mp'=2] {'dp'}, dimensions={0} | all-to-all | bytes 5242880 | tf_op jit(solution)/shard_map/all_to_all | solution.py:93
  126.7 26.0 %all-gather.6.cloned.1.call-done = bf16[4608,1280]{1,0:T(8,128)(2,1)} async-done(((bf16[288,1280]{1,0:T(8,128)(2,1)}), bf16[4608,1280]{1,0:T(8,128)(2,1)}) %all-gather.6.cloned.1.call-update) | async-done | bytes 11796496 | tf_op jit(solution)/shard_map/all_gather | solution.py:108
  152.7 8.5 %multiply_convert_fusion.6 = (bf16[128,1280]{0,1:T(8,128)(2,1)S(1)}, f32[128,1280]{0,1:T(8,128)}) fusion(bf16[4608,1280]{1,0:T(8,128)(2,1)} %all-gather.6.cloned.1.call-done, bf16[128,4608]{1,0:T(8,128)(2,1)S(1)} %copy-done.4), kind=kOutput, calls=%fused_computation.54 | convolution fusion | flops 1511424000 | bytes 13959168 | tf_op jit(solution)/shard_map/dot_general | solution.py:118
  166.3 22.4 %reduce-scatter.4.cloned.1.call-done = f32[128,1280]{1,0:T(8,128)} async-done(((f32[128,2560]{1,0:T(8,128)}), f32[128,1280]{1,0:T(8,128)}) %reduce-scatter.4.cloned.1.call-update) | async-done | bytes 655376 | tf_op jit(solution)/shard_map/reduce_scatter | solution.py:122
  190.8 63.8 %all_to_all.59 = bf16[16,4,16,1280]{3,2,1,0:T(8,128)(2,1)S(1)} all-to-all(bf16[16,4,16,1280]{3,2,1,0:T(8,128)(2,1)S(1)} %bitcast.81), channel_id=1, replica_groups=mesh['dp'=16,'mp'=2] {'dp'}, dimensions={0} | all-to-all | bytes 5242880 | tf_op jit(solution)/shard_map/all_to_all | solution.py:93
  263.2 14.8 %fusion.35 = f32[4,256,768]{2,1,0:T(8,128)} fusion(bf16[4,256,2560]{2,1,0:T(8,128)(2,1)} %all-gather.10.cloned.1.call-done, bf16[4,768,2560]{2,1,0:T(8,128)(2,1)} %param.18), kind=kOutput, calls=%fused_computation.69 | convolution fusion | flops 4026531840 | bytes 24117248 | tf_op jit(solution)/shard_map/erd,efd->erf/dot_general | solution.py:136
  277.9 10.0 %all-to-all-done.2 = bf16[128,16,288]{0,2,1:T(8,128)(2,1)S(1)} async-done(((bf16[128,16,288]{0,2,1:T(8,128)(2,1)}), bf16[128,16,288]{0,2,1:T(8,128)(2,1)S(1)}, u32[]{:S(2)}, u32[]{:S(2)}) %all-to-all-start.2) | async-done | bytes 1179680 | tf_op jit(solution)/shard_map/all_to_all | solution.py:106
  289.1 39.7 %all-gather.8.cloned.1.call-done = bf16[4,256,2560]{2,1,0:T(8,128)(2,1)} async-done(((bf16[4,256,1280]{2,1,0:T(8,128)(2,1)}), bf16[4,256,2560]{2,1,0:T(8,128)(2,1)}) %all-gather.8.cloned.1.call-update) | async-done | bytes 5242896 | tf_op jit(solution)/shard_map/all_gather | solution.py:103
  328.8 10.1 %fusion.34 = f32[4,256,768]{2,1,0:T(8,128)S(1)} fusion(bf16[4,256,2560]{2,1,0:T(8,128)(2,1)} %all-gather.8.cloned.1.call-done, bf16[4,2560,768]{2,1,0:T(8,128)(2,1)} %param.16), kind=kOutput, calls=%fused_computation.68 | convolution fusion | flops 4026531840 | bytes 24117248 | tf_op jit(solution)/shard_map/erd,edf->erf/dot_general | solution.py:139
  338.9 12.8 %multiply_convert_fusion.3 = (bf16[4,256,768]{2,1,0:T(8,128)(2,1)S(1)}, f32[4,256,768]{2,1,0:T(8,128)}) fusion(f32[4,256,768]{2,1,0:T(8,128)S(1)} %fusion.34, bf16[4,256,2560]{2,1,0:T(8,128)(2,1)S(1)} %copy-done.9, bf16[4,2560,768]{2,1,0:T(8,128)(2,1)} %param.17), kind=kOutput, calls=%fused_computation.6 | convolution fusion | flops 4031250432 | bytes 28835840 | tf_op jit(solution)/shard_map/erd,edf->erf/dot_general | solution.py:140
  351.7 13.3 %fusion.4 = f32[4,256,2560]{2,1,0:T(8,128)} fusion(bf16[4,2560,768]{2,1,0:T(8,128)(2,1)} %param.16, f32[4,256,768]{2,1,0:T(8,128)} %copy-done.10, f32[4,256,768]{2,1,0:T(8,128)} %fusion.35, f32[4,256,768]{2,1,0:T(8,128)} %get-tuple-element.50), kind=kOutput, calls=%fused_computation.22 | convolution fusion | flops 4034396160 | bytes 35651584 | tf_op jit(solution)/shard_map/erf,edf->erd/dot_general | solution.py:149
  365.0 15.0 %add_convert_fusion = bf16[4,256,2560]{2,1,0:T(8,128)(2,1)} fusion(f32[4,256,2560]{2,1,0:T(8,128)} %fusion.4, bf16[4,2560,768]{2,1,0:T(8,128)(2,1)} %param.17, f32[4,256,768]{2,1,0:T(8,128)} %fusion.35, f32[4,256,768]{2,1,0:T(8,128)} %copy-done.10), kind=kOutput, calls=%fused_computation | convolution fusion | flops 4036493312 | bytes 37748736 | tf_op jit(solution)/shard_map/erf,edf->erd/dot_general | solution.py:150
  380.3 11.5 %convolution_convert_fusion = bf16[4,256,2560]{2,1,0:T(8,128)(2,1)} fusion(bf16[4,256,768]{2,1,0:T(8,128)(2,1)S(1)} %get-tuple-element.30, bf16[4,768,2560]{2,1,0:T(8,128)(2,1)} %param.18), kind=kOutput, calls=%fused_computation.1 | convolution fusion | flops 4029153280 | bytes 22544384 | tf_op jit(solution)/shard_map/erf,efd->erd/dot_general | solution.py:153
  391.8 54.1 %reduce-scatter.6.cloned.1.call-done = bf16[4,256,1280]{2,1,0:T(8,128)(2,1)} async-done(((bf16[4,256,2560]{2,1,0:T(8,128)(2,1)}), bf16[4,256,1280]{2,1,0:T(8,128)(2,1)}) %reduce-scatter.6.cloned.1.call-update) | async-done | bytes 2621456 | tf_op jit(solution)/shard_map/reduce_scatter | solution.py:158
  455.4 50.0 %all-to-all-done.3 = bf16[16,4,16,1280]{3,2,1,0:T(8,128)(2,1)S(1)} async-done(((bf16[16,4,16,1280]{3,2,1,0:T(8,128)(2,1)}), bf16[16,4,16,1280]{3,2,1,0:T(8,128)(2,1)S(1)}, u32[]{:S(2)}, u32[]{:S(2)}) %all-to-all-start.3) | async-done | bytes 2621472 | tf_op jit(solution)/shard_map/all_to_all | solution.py:162
  506.9 12.3 %all_gather.24 = bf16[128,2560]{1,0:T(8,128)(2,1)S(1)} all-gather(bf16[128,1280]{1,0:T(8,128)(2,1)S(1)} %fusion.1), channel_id=1, replica_groups=mesh['dp'=16,'mp'=2] {'mp'}, dimensions={1}, use_global_device_ids=true | all-gather | bytes 983040 | tf_op jit(solution)/shard_map/all_gather | solution.py:103
  528.0 11.7 %all-to-all-start.5 = ((bf16[128,16,160]{0,2,1:T(8,128)(2,1)}), bf16[128,16,160]{0,2,1:T(8,128)(2,1)}, u32[]{:S(2)}, u32[]{:S(2)}) async-start(bf16[128,16,160]{0,2,1:T(8,128)(2,1)} %bitcast.85), calls=%async_computation.8 | async-start | bytes 1310720 | tf_op jit(solution)/shard_map/all_to_all | solution.py:106
  541.6 18.4 %all-to-all-done.5 = bf16[128,16,160]{0,2,1:T(8,128)(2,1)} async-done(((bf16[128,16,160]{0,2,1:T(8,128)(2,1)}), bf16[128,16,160]{0,2,1:T(8,128)(2,1)}, u32[]{:S(2)}, u32[]{:S(2)}) %all-to-all-start.5) | async-done | bytes 655392 | tf_op jit(solution)/shard_map/all_to_all | solution.py:106
  560.0 12.3 %all-to-all-start.4 = ((bf16[16,4,16,1280]{3,2,1,0:T(8,128)(2,1)}), bf16[16,4,16,1280]{3,2,1,0:T(8,128)(2,1)S(1)}, u32[]{:S(2)}, u32[]{:S(2)}) async-start(bf16[16,4,16,1280]{3,2,1,0:T(8,128)(2,1)} %bitcast.75), calls=%async_computation.7 | async-start | bytes 5242880 | tf_op jit(solution)/shard_map/all_to_all | solution.py:162
  576.8 24.7 %all-gather.14.cloned.1.call-done = bf16[2048,1280]{0,1:T(8,128)(2,1)} async-done(((bf16[128,1280]{0,1:T(8,128)(2,1)}), bf16[2048,1280]{0,1:T(8,128)(2,1)}) %all-gather.14.cloned.1.call-update) | async-done | bytes 5242896 | tf_op jit(solution)/shard_map/all_gather | solution.py:134
  608.4 29.5 %all-to-all-done.4 = bf16[16,4,16,1280]{3,2,1,0:T(8,128)(2,1)S(1)} async-done(((bf16[16,4,16,1280]{3,2,1,0:T(8,128)(2,1)}), bf16[16,4,16,1280]{3,2,1,0:T(8,128)(2,1)S(1)}, u32[]{:S(2)}, u32[]{:S(2)}) %all-to-all-start.4) | async-done | bytes 2621472 | tf_op jit(solution)/shard_map/all_to_all | solution.py:162
  639.1 10.4 %all_gather.25 = bf16[128,2560]{1,0:T(8,128)(2,1)S(1)} all-gather(bf16[128,1280]{1,0:T(8,128)(2,1)S(1)} %fusion.3), channel_id=1, replica_groups=mesh['dp'=16,'mp'=2] {'mp'}, dimensions={1}, use_global_device_ids=true | all-gather | bytes 983040 | tf_op jit(solution)/shard_map/all_gather | solution.py:103
  649.5 25.7 %all-gather.12.cloned.1.call-done = bf16[2048,1280]{0,1:T(8,128)(2,1)} async-done(((bf16[128,1280]{0,1:T(8,128)(2,1)}), bf16[2048,1280]{0,1:T(8,128)(2,1)}) %all-gather.12.cloned.1.call-update) | async-done | bytes 5242896 | tf_op jit(solution)/shard_map/all_gather | solution.py:181
  675.2 8.6 %fusion.8 = (bf16[288,1280]{1,0:T(8,128)(2,1)}, f32[288,1280]{1,0:T(8,128)}, f32[288,1280]{1,0:T(8,128)}) fusion(bf16[288,1280]{1,0:T(8,128)(2,1)} %param.14, f32[288,1280]{1,0:T(8,128)} %param.22, f32[288,1280]{1,0:T(8,128)} %param.23, bf16[2048,288]{0,1:T(8,128)(2,1)} %copy_bitcast_fusion.2, bf16[2048,1280]{0,1:T(8,128)(2,1)} %all-gather.12.cloned.1.call-done), kind=kOutput, calls=%fused_computation.26 | convolution fusion | flops 1516216320 | bytes 13795328 | tf_op jit(solution)/shard_map/dot_general | solution.py:59
  (73 shorter events, 58.6 us)
Async XLA Ops:
  7.2 145.5 %all-gather.6.cloned.1.call-start = ((), (), s32[]{:S(2)}) async-start(), calls=%async_computation.9 | async-start | bytes 12533760 | tf_op jit(solution)/shard_map/all_gather | solution.py:108
  7.9 180.8 %reduce-scatter.4.cloned.1.call-start = ((), (), s32[]{:S(2)}) async-start(), calls=%async_computation.10 | async-start | bytes 1966080 | tf_op jit(solution)/shard_map/reduce_scatter | solution.py:122
  9.4 115.6 %copy-start.7 = (f32[64,128]{1,0:T(8,128)}, f32[64,128]{1,0:T(8,128)S(1)}, u32[]{:S(2)}) copy-start(f32[64,128]{1,0:T(8,128)S(1)} %select_reduce_fusion.1) | copy-start | bytes 98308
  9.6 115.4 %copy-start.5 = (s32[64,128]{1,0:T(8,128)}, s32[64,128]{1,0:T(8,128)S(1)}, u32[]{:S(2)}) copy-start(s32[64,128]{1,0:T(8,128)S(1)} %fusion.10) | copy-start | bytes 98308
  125.0 27.7 %copy-start.4 = (bf16[128,4608]{1,0:T(8,128)(2,1)S(1)}, bf16[128,4608]{1,0:T(8,128)(2,1)}, u32[]{:S(2)}) copy-start(bf16[128,4608]{1,0:T(8,128)(2,1)} %param.13) | copy-start | bytes 3538948
  161.1 5.1 copy-start.3
  166.2 96.9 %all-gather.10.cloned.1.call-start = ((), (), s32[]{:S(2)}) async-start(), calls=%async_computation.12 | async-start | bytes 7864320 | tf_op jit(solution)/shard_map/all_gather | solution.py:103
  189.9 138.9 %all-gather.8.cloned.1.call-start = ((), (), s32[]{:S(2)}) async-start(), calls=%async_computation.11 | async-start | bytes 7864320 | tf_op jit(solution)/shard_map/all_gather | solution.py:103
  257.7 30.2 %all-to-all-start.2 = ((bf16[128,16,288]{0,2,1:T(8,128)(2,1)}), bf16[128,16,288]{0,2,1:T(8,128)(2,1)S(1)}, u32[]{:S(2)}, u32[]{:S(2)}) async-start(bf16[128,16,288]{0,2,1:T(8,128)(2,1)} %bitcast.12), calls=%async_computation.3 | async-start | bytes 2359296 | tf_op jit(solution)/shard_map/all_to_all | solution.py:106
  262.9 183.0 %reduce-scatter.6.cloned.1.call-start = ((), (), s32[]{:S(2)}) async-start(), calls=%async_computation.13 | async-start | bytes 7864320 | tf_op jit(solution)/shard_map/reduce_scatter | solution.py:158
  328.8 10.1 %copy-start.9 = (bf16[4,256,2560]{2,1,0:T(8,128)(2,1)S(1)}, bf16[4,256,2560]{2,1,0:T(8,128)(2,1)}, u32[]{:S(2)}) copy-start(bf16[4,256,2560]{2,1,0:T(8,128)(2,1)} %all-gather.8.cloned.1.call-done) | copy-start | bytes 15728644
  338.9 12.8 %copy-start.10 = (f32[4,256,768]{2,1,0:T(8,128)}, f32[4,256,768]{2,1,0:T(8,128)S(1)}, u32[]{:S(2)}) copy-start(f32[4,256,768]{2,1,0:T(8,128)S(1)} %fusion.34) | copy-start | bytes 9437188
  380.0 145.6 %reduce-scatter.8.cloned.1.call-start = ((), (), s32[]{:S(2)}) async-start(), calls=%async_computation.14 | async-start | bytes 7864320 | tf_op jit(solution)/shard_map/reduce_scatter | solution.py:158
  446.0 1.7 copy-start.1
  446.0 155.5 %all-gather.14.cloned.1.call-start = ((), (), s32[]{:S(2)}) async-start(), calls=%async_computation.16 | async-start | bytes 5570560 | tf_op jit(solution)/shard_map/all_gather | solution.py:134
  449.5 5.8 copy-start.6
  449.5 55.9 %all-to-all-start.3 = ((bf16[16,4,16,1280]{3,2,1,0:T(8,128)(2,1)}), bf16[16,4,16,1280]{3,2,1,0:T(8,128)(2,1)S(1)}, u32[]{:S(2)}, u32[]{:S(2)}) async-start(bf16[16,4,16,1280]{3,2,1,0:T(8,128)(2,1)} %bitcast.78), calls=%async_computation.5 | async-start | bytes 5242880 | tf_op jit(solution)/shard_map/all_to_all | solution.py:162
  455.2 220.0 %all-gather.12.cloned.1.call-start = ((), (), s32[]{:S(2)}) async-start(), calls=%async_computation.15 | async-start | bytes 5570560 | tf_op jit(solution)/shard_map/all_gather | solution.py:181
  505.3 14.8 %copy-start.11 = (f32[128,1280]{0,1:T(8,128)S(1)}, f32[128,1280]{0,1:T(8,128)}, u32[]{:S(2)}) copy-start(f32[128,1280]{0,1:T(8,128)} %get-tuple-element.48) | copy-start | bytes 1966084
  519.3 0.8 copy-start.2
  525.6 14.1 %copy-start = (bf16[4,256,1280]{2,1,0:T(8,128)(2,1)S(1)}, bf16[4,256,1280]{2,1,0:T(8,128)(2,1)}, u32[]{:S(2)}) copy-start(bf16[4,256,1280]{2,1,0:T(8,128)(2,1)} %reduce-scatter.8.cloned.1.call-done) | copy-start | bytes 7864324
  528.0 32.0 %all-to-all-start.5 = ((bf16[128,16,160]{0,2,1:T(8,128)(2,1)}), bf16[128,16,160]{0,2,1:T(8,128)(2,1)}, u32[]{:S(2)}, u32[]{:S(2)}) async-start(bf16[128,16,160]{0,2,1:T(8,128)(2,1)} %bitcast.85), calls=%async_computation.8 | async-start | bytes 1310720 | tf_op jit(solution)/shard_map/all_to_all | solution.py:106
  560.0 16.7 %copy-start.8 = (f32[64,128]{1,0:T(8,128)S(1)}, f32[64,128]{1,0:T(8,128)}, u32[]{:S(2)}) copy-start(f32[64,128]{1,0:T(8,128)} %copy-done.7) | copy-start | bytes 98308
  560.0 77.9 %all-to-all-start.4 = ((bf16[16,4,16,1280]{3,2,1,0:T(8,128)(2,1)}), bf16[16,4,16,1280]{3,2,1,0:T(8,128)(2,1)S(1)}, u32[]{:S(2)}, u32[]{:S(2)}) async-start(bf16[16,4,16,1280]{3,2,1,0:T(8,128)(2,1)} %bitcast.75), calls=%async_computation.7 | async-start | bytes 5242880 | tf_op jit(solution)/shard_map/all_to_all | solution.py:162
Sparse Core Ops, SparseCore 0:
  10.3 142.3 all-gather.5
  166.4 22.3 reduce-scatter.3
  190.3 68.5 all-gather.9
  260.2 68.5 all-gather.7
  380.2 65.7 reduce-scatter.5
  448.1 67.0 reduce-scatter.7
  517.9 83.5 all-gather.13
  604.2 70.9 all-gather.11
